TPU v7x, 32 devices: a whole 2x2x4 slice. The times are simulated.
32 devices in a mesh: slab: 2 (over x), cell: 8 (over z, y), dp: 2 (over core).
Axes of the slice: x: 2, y: 2, z: 4, core: 2. Of those that a mesh axis runs over, the one named last changes fastest.
Arguments:
- sens: float32 [2, 2048, 32768], P(None, ('slab', 'dp'), 'cell'), parts along dimension 1, may hold values from -0.03125 to 0.03125
- observed: float32 [2, 2048], P(None, ('slab', 'dp')), parts along dimension 1, may hold values from -6 to 6
- noise: float32 [2, 2048], P(None, ('slab', 'dp')), parts along dimension 1, may hold values from 0.5 to 2
- survey_ids: int32 [2, 2048], P(None, ('slab', 'dp')), parts along dimension 1, may hold values from 0 to 7
- data_perturb: float32 [2, 8, 2048], P(None, None, ('slab', 'dp')), parts along dimension 2, may hold values from -6 to 6
- prior: float32 [2, 16, 32, 1024], P(None, 'slab', 'cell'), parts along dimension 1, may hold values from -6 to 6
Outputs:
- models: float32 [2, 16, 32, 1024], P(None, 'slab', 'cell'), parts along dimension 1
There are 2 independent parts, one for each index of `slab`. A program takes and returns all parts, laid end to end along the dimension named above; each array names one. Nothing has to cross between parts.
All inputs are finite; a program needn't handle non-finite values.
Results may differ from a plain program's by a relative error of at most 0.0001.
Values sent between devices are 32-bit elements; how exact they have to be, the bound alone decides.
A program may use at most 64 MiB of HBM per device.

v0:
```python
import functools

import jax
import jax.numpy as jnp
from jax import lax
from jax.experimental import pallas as pl
from jax.experimental.pallas import tpu as pltpu
from jax.sharding import PartitionSpec as P

NX = 32
NZ = 32
NSURV = 8
ITERS = 4
LANES = 128

nu_value = 4.0
step_size = 0.5
couple_weight = 0.02
prior_weight = 0.1

MESH = pl.DeviceIdType.MESH


def split_rows(value):
    high = value.astype(jnp.bfloat16).astype(jnp.float32)
    return jnp.concatenate([high, value - high], axis=0).astype(jnp.bfloat16)


def fold_rows(value):
    half = value.shape[0] // 2
    return value[:half] + value[half:]


def cross_gradients(first, second, masks, layer_cells, z_on):
    along_x, along_y = masks

    def differences(field, deeper):
        diff_x = (pltpu.roll(field, layer_cells - 1, 1) - field) * along_x
        diff_y = (pltpu.roll(field, layer_cells - NX, 1) - field) * along_y
        return diff_x, diff_y, (deeper - field) * z_on

    a = differences(*first)
    b = differences(*second)
    tx = a[1] * b[2] - a[2] * b[1]
    ty = a[2] * b[0] - a[0] * b[2]
    tz = a[0] * b[1] - a[1] * b[0]
    scaling = 2.0 / (1.0 + tx * tx + ty * ty + tz * tz)
    sx = scaling * along_x
    sy = scaling * along_y
    sz = scaling * z_on
    return (
        (sx * (b[1] * tz - b[2] * ty), sy * (b[2] * tx - b[0] * tz), sz * (b[0] * ty - b[1] * tx)),
        (sx * (ty * a[2] - tz * a[1]), sy * (tz * a[0] - tx * a[2]), sz * (tx * a[1] - ty * a[0])),
    )


def kernel(
    cells, sens, observed, noise, survey_ids, perturb, prior, out,
    raw, high, low, high_t, low_t, base, carry_z, halo_up, halo_dn, acc, gather, target, per_noise, resids,
    count_tile, sums_mine, sums_other, rows, grad_mine, grad_other,
    load_sem, halo_send, halo_recv, part_send, part_recv, sums_send, sums_recv, grad_send, grad_recv,
):
    stations = observed.shape[1]
    layers, layer_cells = prior.shape[1], prior.shape[3]
    tiles = stations // LANES
    slab = lax.axis_index("slab")
    me = lax.axis_index("cell")
    dp = lax.axis_index("dp")
    partner = 1 - dp

    def load(s, l):
        return pltpu.make_async_copy(
            sens.at[s, :, pl.ds(pl.multiple_of(l * layer_cells, LANES), layer_cells)], raw.at[s, l],
            load_sem.at[s, l],
        )

    for s in range(2):
        for l in range(layers):
            load(s, l).start()

    barrier = pltpu.get_barrier_semaphore()
    pl.semaphore_signal(barrier, inc=1, device_id=(slab, me, partner), device_id_type=MESH)
    for k in range(1, cells):
        there = lax.rem(me + k, cells)
        pl.semaphore_signal(barrier, inc=1, device_id=(slab, there, dp), device_id_type=MESH)

    position = lax.broadcasted_iota(jnp.int32, (1, layer_cells), 1)
    masks = (
        (lax.rem(position, NX) < NX - 1).astype(jnp.float32),
        (position < layer_cells - NX).astype(jnp.float32),
    )
    lane = lax.broadcasted_iota(jnp.int32, (8, LANES), 1)

    @pl.when(me == cells - 1)
    def _():
        halo_up[...] = jnp.zeros_like(halo_up)

    @pl.when(me == 0)
    def _():
        halo_dn[...] = jnp.zeros_like(halo_dn)

    def ids_at(s, t):
        return jnp.broadcast_to(survey_ids[s : s + 1, t * LANES : (t + 1) * LANES], (8, LANES))

    def by_survey(s, values, offset):
        total = jnp.zeros((8, LANES), jnp.float32)
        ids = [ids_at(s, t) for t in range(tiles)]
        for j in range(NSURV):
            one = jnp.where(ids[0] == j, values[0], 0.0)
            for t in range(1, tiles):
                one = one + jnp.where(ids[t] == j, values[t], 0.0)
            total = jnp.where(lane == j + offset, jnp.sum(one, axis=1, keepdims=True), total)
        return total

    for s in range(2):
        count_tile[s] = by_survey(s, [jnp.ones((8, LANES), jnp.float32)] * tiles, NSURV)
        scale = noise[s : s + 1]
        target[s] = observed[s : s + 1] + scale * perturb[s]
        per_noise[s] = jnp.broadcast_to(1.0 / scale, per_noise.shape[1:])

    def halo_copy(source, it, s, up):
        return pltpu.make_async_remote_copy(
            src_ref=source.at[s, 0 if up else layers - 1],
            dst_ref=(halo_up if up else halo_dn).at[it, s],
            send_sem=halo_send.at[s, 0 if up else 1],
            recv_sem=halo_recv.at[it, s, 0 if up else 1],
            device_id=(slab, jnp.maximum(me - 1, 0) if up else jnp.minimum(me + 1, cells - 1), dp),
            device_id_type=MESH,
        )

    def start_halo(source, it, s, l):
        if l == 0:
            @pl.when(me > 0)
            def _():
                halo_copy(source, it, s, True).start()

        if l == layers - 1:
            @pl.when(me < cells - 1)
            def _():
                halo_copy(source, it, s, False).start()

    def wait_halo_sent(source, it, s):
        @pl.when(me > 0)
        def _():
            halo_copy(source, it, s, True).wait_send()

        @pl.when(me < cells - 1)
        def _():
            halo_copy(source, it, s, False).wait_send()

    def wait_halo_here(source, it, s):
        @pl.when(me < cells - 1)
        def _():
            halo_copy(source, it, s, True).wait_recv()

        @pl.when(me > 0)
        def _():
            halo_copy(source, it, s, False).wait_recv()

    def send_parts(it, s):
        gather[it, s, me] = fold_rows(acc[...])
        for k in range(1, cells):
            pltpu.make_async_remote_copy(
                src_ref=gather.at[it, s, me], dst_ref=gather.at[it, s, me],
                send_sem=part_send.at[s], recv_sem=part_recv.at[it, s],
                device_id=(slab, lax.rem(me + k, cells), dp), device_id_type=MESH,
            ).start()

    def wait_parts_sent(it, s):
        sent = gather.at[it, s, pl.ds(0, cells - 1)]
        pltpu.make_async_copy(sent, sent, part_send.at[s]).wait()

    def sums_copy(it, s):
        return pltpu.make_async_remote_copy(
            src_ref=sums_mine.at[it, s], dst_ref=sums_other.at[it, s],
            send_sem=sums_send.at[s], recv_sem=sums_recv.at[it, s],
            device_id=(slab, me, partner), device_id_type=MESH,
        )

    def residuals(it, s):
        got = gather.at[it, s, pl.ds(0, cells - 1)]
        pltpu.make_async_copy(got, got, part_recv.at[it, s]).wait()
        squares = []
        for t in range(tiles):
            span = slice(t * LANES, (t + 1) * LANES)
            predicted = gather[it, s, 0, :, span]
            for c in range(1, cells):
                predicted = predicted + gather[it, s, c, :, span]
            resid = (predicted - target[s, :, span]) * per_noise[s, :, span]
            resids[s, :, span] = resid
            squares.append(resid * resid)
        sums_mine[it, s] = by_survey(s, squares, 0) + count_tile[s]
        sums_copy(it, s).start()

    def weigh(it, s):
        sums_copy(it, s).wait_recv()
        sums = sums_mine[it, s] + sums_other[it, s]
        counts = pltpu.roll(sums, LANES - NSURV, 1)
        per_root = lax.rsqrt((sums + 1.0) / (counts + 1.0))
        columns = [jnp.broadcast_to(per_root[:, j : j + 1], (8, LANES)) for j in range(NSURV)]
        for t in range(tiles):
            span = slice(t * LANES, (t + 1) * LANES)
            ids = ids_at(s, t)
            per_scale = columns[0]
            for j in range(1, NSURV):
                per_scale = jnp.where(ids == j, columns[j], per_scale)
            whitened = resids[s, :, span] * per_scale
            factor = (
                (nu_value + 1.0) * whitened * (per_noise[s, :, span] * per_scale)
                / (nu_value + whitened * whitened)
            )
            rows[s, :, span] = split_rows(factor)

    def grad_copy(it, s, l):
        return pltpu.make_async_remote_copy(
            src_ref=grad_mine.at[s, l], dst_ref=grad_other.at[it, s, l],
            send_sem=grad_send.at[s, l], recv_sem=grad_recv.at[it, s, l],
            device_id=(slab, me, partner), device_id_type=MESH,
        )

    def gradient(it, s):
        for l in range(layers):
            factor = rows[s]
            product = jnp.dot(factor, high[s, l], preferred_element_type=jnp.float32)
            product = product + jnp.dot(factor, low[s, l], preferred_element_type=jnp.float32)
            grad_mine[s, l] = fold_rows(product)
            grad_copy(it, s, l).start()

    def predict(s, l, value):
        model = split_rows(value)
        product = jnp.dot(model, high_t[s, l], preferred_element_type=jnp.float32)
        product = product + jnp.dot(model, low_t[s, l], preferred_element_type=jnp.float32)
        acc[...] += product

    def couple(source, it):
        for l in range(layers):
            if l == 0:
                z_on = (me > 0).astype(jnp.float32)
                first, second = [(halo_dn[it, s], source[s, 0]) for s in range(2)]
                ga, gb = cross_gradients(first, second, masks, layer_cells, z_on)
                carry_z[0] = ga[2]
                carry_z[1] = gb[2]
            z_on = (me * layers + l < NZ - 1).astype(jnp.float32)
            first, second = [
                (source[s, l], source[s, l + 1] if l < layers - 1 else halo_up[it, s]) for s in range(2)
            ]
            both = cross_gradients(first, second, masks, layer_cells, z_on)
            for s in range(2):
                gx, gy, gz = both[s]
                total = pltpu.roll(gx, 1, 1) - gx + (pltpu.roll(gy, NX, 1) - gy) + (carry_z[s] - gz)
                carry_z[s] = gz
                field = source[s, l]
                base[s, l] = field - step_size * (
                    couple_weight * total + prior_weight * (field - prior[s, l])
                )

    def step(source, it, last):
        for s in range(2):
            residuals(it, s)
            if s == 0:
                for other in range(2):
                    wait_halo_here(source, it, other)
                couple(source, it)
            weigh(it, s)
            gradient(it, s)
            wait_halo_sent(source, it, s)
            acc[...] = jnp.zeros_like(acc)
            for l in range(layers):
                grad_copy(it, s, l).wait_recv()
                value = base[s, l] - step_size * (grad_mine[s, l] + grad_other[it, s, l])
                out[s, l] = value
                if not last:
                    start_halo(out, it + 1, s, l)
                    predict(s, l, value)
            wait_parts_sent(it, s)
            if not last:
                send_parts(it + 1, s)
            sums_copy(it, s).wait_send()
            for l in range(layers):
                grad_copy(it, s, l).wait_send()

    pl.semaphore_wait(barrier, cells)
    for s in range(2):
        for l in range(layers):
            start_halo(prior, 0, s, l)
    for s in range(2):
        acc[...] = jnp.zeros_like(acc)

        @pl.loop(0, layers)
        def _(l, s=s):
            load(s, l).wait()
            value = raw[s, l]
            rounded = value.astype(jnp.bfloat16)
            high[s, l] = rounded
            low[s, l] = (value - rounded.astype(jnp.float32)).astype(jnp.bfloat16)
            high_t[s, l] = high[s, l].T
            low_t[s, l] = low[s, l].T
            predict(s, l, prior[s, l])

        send_parts(0, s)

    step(prior, 0, ITERS == 1)
    if ITERS > 2:
        @pl.loop(1, ITERS - 1)
        def _(it):
            step(out, it, False)
    if ITERS > 1:
        step(out, ITERS - 1, True)


def body(sens, observed, noise, survey_ids, data_perturb, prior):
    cells = lax.axis_size("cell")
    models, layers, layer_cells = prior.shape[1:]
    stations = observed.shape[1]
    tiles = stations // LANES
    assert models == 8 and stations % LANES == 0
    assert lax.axis_size("dp") == 2
    f32, bf16 = jnp.float32, jnp.bfloat16
    field = (2, layers, models, layer_cells)
    vmem = pl.BlockSpec(memory_space=pltpu.VMEM)
    dma = pltpu.SemaphoreType.DMA
    out = pl.pallas_call(
        functools.partial(kernel, cells),
        out_shape=jax.ShapeDtypeStruct(field, f32),
        in_specs=[pl.BlockSpec(memory_space=pl.ANY)] + [vmem] * 5,
        out_specs=vmem,
        scratch_shapes=[
            pltpu.VMEM((2, layers, stations, layer_cells), f32),
            pltpu.VMEM((2, layers, stations, layer_cells), bf16),
            pltpu.VMEM((2, layers, stations, layer_cells), bf16),
            pltpu.VMEM((2, layers, layer_cells, stations), bf16),
            pltpu.VMEM((2, layers, layer_cells, stations), bf16),
            pltpu.VMEM(field, f32),
            pltpu.VMEM((2, models, layer_cells), f32),
            pltpu.VMEM((ITERS, 2, models, layer_cells), f32),
            pltpu.VMEM((ITERS, 2, models, layer_cells), f32),
            pltpu.VMEM((2 * models, stations), f32),
            pltpu.VMEM((ITERS, 2, cells, models, stations), f32),
            pltpu.VMEM((2, models, stations), f32),
            pltpu.VMEM((2, models, stations), f32),
            pltpu.VMEM((2, models, stations), f32),
            pltpu.VMEM((2, models, LANES), f32),
            pltpu.VMEM((ITERS, 2, models, LANES), f32),
            pltpu.VMEM((ITERS, 2, models, LANES), f32),
            pltpu.VMEM((2, 2 * models, stations), bf16),
            pltpu.VMEM(field, f32),
            pltpu.VMEM((ITERS,) + field, f32),
            dma((2, layers)),
            dma((2, 2)),
            dma((ITERS, 2, 2)),
            dma((2,)),
            dma((ITERS, 2)),
            dma((2,)),
            dma((ITERS, 2)),
            dma((2, layers)),
            dma((ITERS, 2, layers)),
        ],
        compiler_params=pltpu.CompilerParams(
            collective_id=0, has_side_effects=True, vmem_limit_bytes=60 * 1024 * 1024
        ),
    )(sens, observed, noise, survey_ids, data_perturb, prior.transpose(0, 2, 1, 3))
    return out.transpose(0, 2, 1, 3)


def solution(mesh):
    return jax.shard_map(
        body,
        mesh=mesh,
        in_specs=(
            P(None, ("slab", "dp"), "cell"),
            P(None, ("slab", "dp")),
            P(None, ("slab", "dp")),
            P(None, ("slab", "dp")),
            P(None, None, ("slab", "dp")),
            P(None, "slab", "cell", None),
        ),
        out_specs=P(None, "slab", "cell", None),
        check_vma=False,
    )
```

profile of v0, /device:TPU:0, one launch (start us, length us, event | category | flops | bytes accessed | tf_op | source)
XLA Modules:
  0.0 58.9 jit_solution(12695385672391795117)
XLA Ops:
  0.0 1.8 %copy.10 = f32[2,8,4,1024]{3,1,2,0:T(8,128)} copy(f32[2,8,4,1024]{3,2,1,0:T(4,128)} %param.11) | data formatting | bytes 524288 | tf_op args[5]
  1.8 55.3 %shard_map.64 = f32[2,4,8,1024]{3,2,1,0:T(8,128)} custom-call(f32[2,512,4096]{2,1,0:T(8,128)} %sens.1, f32[2,512]{1,0:T(2,128)} %observed.1, f32[2,512]{1,0:T(2,128)} %noise.1, s32[2,512]{1,0:T(2,128)} %survey_ids.1, f32[2,8,512]{2,1,0:T(8,128)} %perturb.1, f32[2,4,8,1024]{3,2,1,0:T(8,128)} %bitcast.5), custom_call_target="tpu_custom_call" | custom-call | tf_op jit(solution)/shard_map/pallas_call | solution.py:322
  57.1 1.8 %copy.8 = f32[2,8,4,1024]{3,2,1,0:T(4,128)} copy(f32[2,8,4,1024]{3,1,2,0:T(8,128)} %bitcast.4) | data formatting | bytes 524288 | tf_op jit(solution)/shard_map/transpose | solution.py:362
where the time goes:
time: 59.1 us; the launch traced here: 58.9 us
  Pallas kernels  55.3 us (94%)
  local copies, waits for them, and re-layouts  3.63 us (6%)
    pallas_call x1, Pallas kernels, body(): pl.pallas_call(functools.partial(kernel, cells), out_shape=jax.ShapeDtype...  55.3 us
    transpose x1, local copies, waits for them, and re-layouts, body(): return out.transpose(0, 2, 1, 3)  1.82 us
    unnamed x1, local copies, waits for them, and re-layouts  1.81 us

commit v1 on v0

--- a/solution.py
+++ b/solution.py
@@ -12,6 +12,8 @@
 NSURV = 8
 ITERS = 4
 LANES = 128
+MODELS = 8
+PARTS = 2
 
 nu_value = 4.0
 step_size = 0.5
@@ -55,18 +57,22 @@
 
 
 def kernel(
-    cells, sens, observed, noise, survey_ids, perturb, prior, out,
-    raw, high, low, high_t, low_t, base, carry_z, halo_up, halo_dn, acc, gather, target, per_noise, resids,
+    cells, layers, sens, observed_in, noise_in, ids_in, perturb_in, prior_in, result,
+    observed, noise, survey_ids, perturb, prior_raw, prior, out, raw, high, low, high_t, low_t, base, carry_z, halo_up, halo_dn, acc, gather, target, per_noise, resids,
     count_tile, sums_mine, sums_other, rows, grad_mine, grad_other,
-    load_sem, halo_send, halo_recv, part_send, part_recv, sums_send, sums_recv, grad_send, grad_recv,
+    input_sem, load_sem, halo_send, halo_recv, part_send, part_recv, sums_send, sums_recv, grad_send, grad_recv,
 ):
     stations = observed.shape[1]
-    layers, layer_cells = prior.shape[1], prior.shape[3]
+    layer_cells = prior.shape[3]
+    blocks = layer_cells // LANES
     tiles = stations // LANES
     slab = lax.axis_index("slab")
     me = lax.axis_index("cell")
     dp = lax.axis_index("dp")
     partner = 1 - dp
+    width = layer_cells // PARTS
+    order = sorted(range(layers), key=lambda l: 0 < l < layers - 1)
+    pieces = [(l, slice(h * width, (h + 1) * width)) for l in order for h in range(PARTS)]
 
     def load(s, l):
         return pltpu.make_async_copy(
@@ -74,9 +80,17 @@
             load_sem.at[s, l],
         )
 
-    for s in range(2):
-        for l in range(layers):
-            load(s, l).start()
+    inputs = [
+        pltpu.make_async_copy(source, kept, input_sem.at[i])
+        for i, (source, kept) in enumerate((
+            (prior_in, prior_raw), (observed_in, observed), (noise_in, noise), (ids_in, survey_ids),
+            (perturb_in, perturb),
+        ))
+    ]
+    for copy in inputs:
+        copy.start()
+    for n in range(min(2, 2 * layers)):
+        load(n // layers, n % layers).start()
 
     barrier = pltpu.get_barrier_semaphore()
     pl.semaphore_signal(barrier, inc=1, device_id=(slab, me, partner), device_id_type=MESH)
@@ -98,6 +112,16 @@
     @pl.when(me == 0)
     def _():
         halo_dn[...] = jnp.zeros_like(halo_dn)
+
+    def rows_of(l, j):
+        return pl.ds(j * layers + l, MODELS, stride=blocks * layers)
+
+    for copy in inputs:
+        copy.wait()
+    for s in range(2):
+        for l in range(layers):
+            for j in range(blocks):
+                prior[s, l, :, j * LANES : (j + 1) * LANES] = prior_raw[s, rows_of(l, j), :]
 
     def ids_at(s, t):
         return jnp.broadcast_to(survey_ids[s : s + 1, t * LANES : (t + 1) * LANES], (8, LANES))
@@ -148,17 +172,19 @@
         def _():
             halo_copy(source, it, s, False).wait_send()
 
-    def wait_halo_here(source, it, s):
+    def wait_halos_here(source, it):
         @pl.when(me < cells - 1)
         def _():
-            halo_copy(source, it, s, True).wait_recv()
+            for s in range(2):
+                halo_copy(source, it, s, True).wait_recv()
 
         @pl.when(me > 0)
         def _():
-            halo_copy(source, it, s, False).wait_recv()
-
-    def send_parts(it, s):
-        gather[it, s, me] = fold_rows(acc[...])
+            for s in range(2):
+                halo_copy(source, it, s, False).wait_recv()
+
+    def send_parts(it, s, total):
+        gather[it, s, me] = fold_rows(total)
         for k in range(1, cells):
             pltpu.make_async_remote_copy(
                 src_ref=gather.at[it, s, me], dst_ref=gather.at[it, s, me],
@@ -211,73 +237,95 @@
             )
             rows[s, :, span] = split_rows(factor)
 
-    def grad_copy(it, s, l):
+    def grad_copy(it, s, p):
         return pltpu.make_async_remote_copy(
-            src_ref=grad_mine.at[s, l], dst_ref=grad_other.at[it, s, l],
-            send_sem=grad_send.at[s, l], recv_sem=grad_recv.at[it, s, l],
+            src_ref=grad_mine.at[s, p], dst_ref=grad_other.at[it, s, p],
+            send_sem=grad_send.at[s, p], recv_sem=grad_recv.at[it, s, p],
             device_id=(slab, me, partner), device_id_type=MESH,
         )
 
-    def gradient(it, s):
-        for l in range(layers):
-            factor = rows[s]
-            product = jnp.dot(factor, high[s, l], preferred_element_type=jnp.float32)
-            product = product + jnp.dot(factor, low[s, l], preferred_element_type=jnp.float32)
-            grad_mine[s, l] = fold_rows(product)
-            grad_copy(it, s, l).start()
-
-    def predict(s, l, value):
+    def gradient(it, s, beside):
+        factor = rows[s]
+
+        def finish(p, product):
+            grad_mine[s, p] = fold_rows(product)
+            grad_copy(it, s, p).start()
+
+        held = None
+        for p, (l, span) in enumerate(pieces):
+            product = jnp.dot(factor, high[s, l, :, span], preferred_element_type=jnp.float32)
+            product = product + jnp.dot(factor, low[s, l, :, span], preferred_element_type=jnp.float32)
+            beside(p)
+            if held is not None:
+                finish(p - 1, held)
+            held = product
+        finish(len(pieces) - 1, held)
+
+    def predict(s, l, span, value):
         model = split_rows(value)
-        product = jnp.dot(model, high_t[s, l], preferred_element_type=jnp.float32)
-        product = product + jnp.dot(model, low_t[s, l], preferred_element_type=jnp.float32)
-        acc[...] += product
-
-    def couple(source, it):
-        for l in range(layers):
-            if l == 0:
-                z_on = (me > 0).astype(jnp.float32)
-                first, second = [(halo_dn[it, s], source[s, 0]) for s in range(2)]
-                ga, gb = cross_gradients(first, second, masks, layer_cells, z_on)
-                carry_z[0] = ga[2]
-                carry_z[1] = gb[2]
-            z_on = (me * layers + l < NZ - 1).astype(jnp.float32)
-            first, second = [
-                (source[s, l], source[s, l + 1] if l < layers - 1 else halo_up[it, s]) for s in range(2)
-            ]
+        product = jnp.dot(model, high_t[s, l, span], preferred_element_type=jnp.float32)
+        return product + jnp.dot(model, low_t[s, l, span], preferred_element_type=jnp.float32)
+
+    def couple(source, it, l):
+        if l == layers - 1:
+            wait_halos_here(source, it)
+        z_on = (me * layers + l < NZ - 1).astype(jnp.float32)
+        first, second = [
+            (source[s, l], source[s, l + 1] if l < layers - 1 else halo_up[it, s]) for s in range(2)
+        ]
+        both = cross_gradients(first, second, masks, layer_cells, z_on)
+        for s in range(2):
+            gx, gy, gz = both[s]
+            total = pltpu.roll(gx, 1, 1) - gx + (pltpu.roll(gy, NX, 1) - gy) - gz
+            if l > 0:
+                total = total + carry_z[s]
+            carry_z[s] = gz
+            field = source[s, l]
+            base[s, l] = field - step_size * (
+                couple_weight * total + prior_weight * (field - prior[s, l])
+            )
+        if l == layers - 1:
+            z_on = (me > 0).astype(jnp.float32)
+            first, second = [(halo_dn[it, s], source[s, 0]) for s in range(2)]
             both = cross_gradients(first, second, masks, layer_cells, z_on)
             for s in range(2):
-                gx, gy, gz = both[s]
-                total = pltpu.roll(gx, 1, 1) - gx + (pltpu.roll(gy, NX, 1) - gy) + (carry_z[s] - gz)
-                carry_z[s] = gz
-                field = source[s, l]
-                base[s, l] = field - step_size * (
-                    couple_weight * total + prior_weight * (field - prior[s, l])
-                )
+                base[s, 0] -= step_size * couple_weight * both[s][2]
+
+    def advance(source, it, s, last):
+        wait_halo_sent(source, it, s)
+        total = jnp.zeros((2 * MODELS, stations), jnp.float32)
+        for p, (l, span) in enumerate(pieces):
+            grad_copy(it, s, p).wait_recv()
+            value = base[s, l, :, span] - step_size * (grad_mine[s, p] + grad_other[it, s, p])
+            if last:
+                for j in range(width // LANES):
+                    result[s, rows_of(l, span.start // LANES + j), :] = value[:, j * LANES : (j + 1) * LANES]
+            else:
+                out[s, l, :, span] = value
+                if p % PARTS == PARTS - 1:
+                    start_halo(out, it + 1, s, l)
+                total = total + predict(s, l, span, value)
+        wait_parts_sent(it, s)
+        if not last:
+            send_parts(it + 1, s, total)
+        sums_copy(it, s).wait_send()
+        for p in range(len(pieces)):
+            grad_copy(it, s, p).wait_send()
 
     def step(source, it, last):
-        for s in range(2):
-            residuals(it, s)
-            if s == 0:
-                for other in range(2):
-                    wait_halo_here(source, it, other)
-                couple(source, it)
-            weigh(it, s)
-            gradient(it, s)
-            wait_halo_sent(source, it, s)
-            acc[...] = jnp.zeros_like(acc)
-            for l in range(layers):
-                grad_copy(it, s, l).wait_recv()
-                value = base[s, l] - step_size * (grad_mine[s, l] + grad_other[it, s, l])
-                out[s, l] = value
-                if not last:
-                    start_halo(out, it + 1, s, l)
-                    predict(s, l, value)
-            wait_parts_sent(it, s)
-            if not last:
-                send_parts(it + 1, s)
-            sums_copy(it, s).wait_send()
-            for l in range(layers):
-                grad_copy(it, s, l).wait_send()
+        residuals(it, 0)
+        weigh(it, 0)
+
+        def beside(p):
+            if p % PARTS == 0:
+                couple(source, it, p // PARTS)
+
+        gradient(it, 0, beside)
+        advance(source, it, 0, last)
+        residuals(it, 1)
+        weigh(it, 1)
+        gradient(it, 1, lambda p: None)
+        advance(source, it, 1, last)
 
     pl.semaphore_wait(barrier, cells)
     for s in range(2):
@@ -289,15 +337,21 @@
         @pl.loop(0, layers)
         def _(l, s=s):
             load(s, l).wait()
+            later = s * layers + l + 2
+
+            @pl.when(later < 2 * layers)
+            def _():
+                load(later // layers, lax.rem(later, layers)).start()
+
             value = raw[s, l]
             rounded = value.astype(jnp.bfloat16)
             high[s, l] = rounded
             low[s, l] = (value - rounded.astype(jnp.float32)).astype(jnp.bfloat16)
             high_t[s, l] = high[s, l].T
             low_t[s, l] = low[s, l].T
-            predict(s, l, prior[s, l])
-
-        send_parts(0, s)
+            acc[...] += predict(s, l, slice(0, layer_cells), prior[s, l])
+
+        send_parts(0, s, acc[...])
 
     step(prior, 0, ITERS == 1)
     if ITERS > 2:
@@ -313,18 +367,29 @@
     models, layers, layer_cells = prior.shape[1:]
     stations = observed.shape[1]
     tiles = stations // LANES
-    assert models == 8 and stations % LANES == 0
+    pieces, width = layers * PARTS, layer_cells // PARTS
+    assert models == MODELS and stations % LANES == 0 and width % LANES == 0
     assert lax.axis_size("dp") == 2
     f32, bf16 = jnp.float32, jnp.bfloat16
     field = (2, layers, models, layer_cells)
+    blocks = layer_cells // LANES
+    flat = (2, models * blocks * layers, LANES)
     vmem = pl.BlockSpec(memory_space=pltpu.VMEM)
     dma = pltpu.SemaphoreType.DMA
+    prior = prior.reshape(2, models, layers, blocks, LANES).transpose(0, 1, 3, 2, 4).reshape(flat)
     out = pl.pallas_call(
-        functools.partial(kernel, cells),
-        out_shape=jax.ShapeDtypeStruct(field, f32),
-        in_specs=[pl.BlockSpec(memory_space=pl.ANY)] + [vmem] * 5,
+        functools.partial(kernel, cells, layers),
+        out_shape=jax.ShapeDtypeStruct(flat, f32),
+        in_specs=[pl.BlockSpec(memory_space=pl.ANY)] * 6,
         out_specs=vmem,
         scratch_shapes=[
+            pltpu.VMEM((2, stations), f32),
+            pltpu.VMEM((2, stations), f32),
+            pltpu.VMEM((2, stations), jnp.int32),
+            pltpu.VMEM((2, models, stations), f32),
+            pltpu.VMEM(flat, f32),
+            pltpu.VMEM(field, f32),
+            pltpu.VMEM(field, f32),
             pltpu.VMEM((2, layers, stations, layer_cells), f32),
             pltpu.VMEM((2, layers, stations, layer_cells), bf16),
             pltpu.VMEM((2, layers, stations, layer_cells), bf16),
@@ -343,8 +408,9 @@
             pltpu.VMEM((ITERS, 2, models, LANES), f32),
             pltpu.VMEM((ITERS, 2, models, LANES), f32),
             pltpu.VMEM((2, 2 * models, stations), bf16),
-            pltpu.VMEM(field, f32),
-            pltpu.VMEM((ITERS,) + field, f32),
+            pltpu.VMEM((2, pieces, models, width), f32),
+            pltpu.VMEM((ITERS, 2, pieces, models, width), f32),
+            dma((5,)),
             dma((2, layers)),
             dma((2, 2)),
             dma((ITERS, 2, 2)),
@@ -352,14 +418,15 @@
             dma((ITERS, 2)),
             dma((2,)),
             dma((ITERS, 2)),
-            dma((2, layers)),
-            dma((ITERS, 2, layers)),
+            dma((2, pieces)),
+            dma((ITERS, 2, pieces)),
         ],
         compiler_params=pltpu.CompilerParams(
-            collective_id=0, has_side_effects=True, vmem_limit_bytes=60 * 1024 * 1024
+            collective_id=0, has_side_effects=True, vmem_limit_bytes=57000 * 1024
         ),
-    )(sens, observed, noise, survey_ids, data_perturb, prior.transpose(0, 2, 1, 3))
-    return out.transpose(0, 2, 1, 3)
+    )(sens, observed, noise, survey_ids, data_perturb, prior)
+    out = out.reshape(2, models, blocks, layers, LANES).transpose(0, 1, 3, 2, 4)
+    return out.reshape(2, models, layers, layer_cells)
 
 
 def solution(mesh):

time: 59.1 us -> 53.1 us (0.90)
  Pallas kernels: 55.3 us -> 51.3 us
  local copies, waits for them, and re-layouts: 3.63 us -> 1.67 us
    pallas_call x1, Pallas kernels: 55.3 us -> 51.3 us  [body(): pl.pallas_call(functools.partial(kernel, cells, layers), out_shape=jax.Sh...]
    transpose x1 -> x0, local copies, waits for them, and re-layouts: 1.82 us -> none  [body(): return out.transpose(0, 2, 1, 3)]
where the time goes in v1:
time: 53.1 us; the launch traced here: 53 us
  Pallas kernels  51.3 us (97%)
  local copies, waits for them, and re-layouts  1.67 us (3%)
    pallas_call x1, Pallas kernels, body(): pl.pallas_call(functools.partial(kernel, cells, layers), out_shape=jax.Sh...  51.3 us
    unnamed x1, local copies, waits for them, and re-layouts  1.67 us

profile of v1, /device:TPU:0, one launch (start us, length us, event | category | flops | bytes accessed | tf_op | source)
XLA Modules:
  0.0 53.0 jit_solution(16042761848640147727)
XLA Ops:
  0.0 51.3 %shard_map.64 = f32[2,256,128]{2,1,0:T(8,128)} custom-call(f32[2,512,4096]{2,1,0:T(8,128)} %sens.1, f32[2,512]{1,0:T(2,128)} %observed_in.1, f32[2,512]{1,0:T(2,128)} %noise_in.1, s32[2,512]{1,0:T(2,128)} %ids_in.1, f32[2,8,512]{2,1,0:T(8,128)} %perturb_in.1, f32[2,256,128]{2,1,0:T(8,128)} %bitcast.11), custom_call_target="tpu_custom_call" | custom-call | tf_op jit(solution)/shard_map/pallas_call | solution.py:380
  51.3 1.7 %copy.10 = f32[2,8,4,1024]{3,2,1,0:T(4,128)} copy(f32[2,8,4,1024]{3,2,1,0:T(4,128)} %bitcast.10) | data formatting | bytes 524288

commit v2 on v1

--- a/solution.py
+++ b/solution.py
@@ -13,7 +13,7 @@
 ITERS = 4
 LANES = 128
 MODELS = 8
-PARTS = 2
+PARTS = 1
 
 nu_value = 4.0
 step_size = 0.5
@@ -57,10 +57,10 @@
 
 
 def kernel(
-    cells, layers, sens, observed_in, noise_in, ids_in, perturb_in, prior_in, result,
-    observed, noise, survey_ids, perturb, prior_raw, prior, out, raw, high, low, high_t, low_t, base, carry_z, halo_up, halo_dn, acc, gather, target, per_noise, resids,
+    cells, layers, sens, observed_in, noise_in, ids_in, perturb_in, prior_in, result_out,
+    observed, noise, survey_ids, perturb, prior_raw, prior, out, result, raw, high, low, high_t, low_t, base, carry_z, halo_up, halo_dn, acc, gather, target, per_noise, resids,
     count_tile, sums_mine, sums_other, rows, grad_mine, grad_other,
-    input_sem, load_sem, halo_send, halo_recv, part_send, part_recv, sums_send, sums_recv, grad_send, grad_recv,
+    input_sem, result_sem, load_sem, halo_send, halo_recv, part_send, part_recv, sums_send, sums_recv, grad_send, grad_recv,
 ):
     stations = observed.shape[1]
     layer_cells = prior.shape[3]
@@ -284,12 +284,13 @@
             base[s, l] = field - step_size * (
                 couple_weight * total + prior_weight * (field - prior[s, l])
             )
-        if l == layers - 1:
-            z_on = (me > 0).astype(jnp.float32)
-            first, second = [(halo_dn[it, s], source[s, 0]) for s in range(2)]
-            both = cross_gradients(first, second, masks, layer_cells, z_on)
-            for s in range(2):
-                base[s, 0] -= step_size * couple_weight * both[s][2]
+
+    def couple_below(source, it):
+        z_on = (me > 0).astype(jnp.float32)
+        first, second = [(halo_dn[it, s], source[s, 0]) for s in range(2)]
+        both = cross_gradients(first, second, masks, layer_cells, z_on)
+        for s in range(2):
+            base[s, 0] -= step_size * couple_weight * both[s][2]
 
     def advance(source, it, s, last):
         wait_halo_sent(source, it, s)
@@ -308,17 +309,23 @@
         wait_parts_sent(it, s)
         if not last:
             send_parts(it + 1, s, total)
+        if last:
+            pltpu.make_async_copy(result.at[s], result_out.at[s], result_sem.at[s]).start()
         sums_copy(it, s).wait_send()
         for p in range(len(pieces)):
             grad_copy(it, s, p).wait_send()
 
     def step(source, it, last):
         residuals(it, 0)
+        for l in range(layers - 1):
+            couple(source, it, l)
         weigh(it, 0)
 
         def beside(p):
-            if p % PARTS == 0:
-                couple(source, it, p // PARTS)
+            if p == max(len(pieces) - 4, 0):
+                couple(source, it, layers - 1)
+            if p == len(pieces) - 2:
+                couple_below(source, it)
 
         gradient(it, 0, beside)
         advance(source, it, 0, last)
@@ -360,6 +367,8 @@
             step(out, it, False)
     if ITERS > 1:
         step(out, ITERS - 1, True)
+    for s in range(2):
+        pltpu.make_async_copy(result.at[s], result_out.at[s], result_sem.at[s]).wait()
 
 
 def body(sens, observed, noise, survey_ids, data_perturb, prior):
@@ -381,7 +390,7 @@
         functools.partial(kernel, cells, layers),
         out_shape=jax.ShapeDtypeStruct(flat, f32),
         in_specs=[pl.BlockSpec(memory_space=pl.ANY)] * 6,
-        out_specs=vmem,
+        out_specs=pl.BlockSpec(memory_space=pl.ANY),
         scratch_shapes=[
             pltpu.VMEM((2, stations), f32),
             pltpu.VMEM((2, stations), f32),
@@ -390,6 +399,7 @@
             pltpu.VMEM(flat, f32),
             pltpu.VMEM(field, f32),
             pltpu.VMEM(field, f32),
+            pltpu.VMEM(flat, f32),
             pltpu.VMEM((2, layers, stations, layer_cells), f32),
             pltpu.VMEM((2, layers, stations, layer_cells), bf16),
             pltpu.VMEM((2, layers, stations, layer_cells), bf16),
@@ -411,6 +421,7 @@
             pltpu.VMEM((2, pieces, models, width), f32),
             pltpu.VMEM((ITERS, 2, pieces, models, width), f32),
             dma((5,)),
+            dma((2,)),
             dma((2, layers)),
             dma((2, 2)),
             dma((ITERS, 2, 2)),

time: 53.1 us -> 52 us (0.979)
  Pallas kernels: 51.3 us -> 50.1 us
    pallas_call x1, Pallas kernels: 51.3 us -> 50.1 us  [body(): pl.pallas_call(functools.partial(kernel, cells, layers), out_shape=jax.Sh...]
where the time goes in v2:
time: 52 us; the launch traced here: 51.8 us
  Pallas kernels  50.1 us (96%)
  local copies, waits for them, and re-layouts  1.67 us (3%)
    pallas_call x1, Pallas kernels, body(): pl.pallas_call(functools.partial(kernel, cells, layers), out_shape=jax.Sh...  50.1 us
    unnamed x1, local copies, waits for them, and re-layouts  1.67 us

profile of v2, /device:TPU:0, one launch (start us, length us, event | category | flops | bytes accessed | tf_op | source)
XLA Modules:
  0.0 51.8 jit_solution(321234777840390528)
XLA Ops:
  0.0 50.1 %shard_map.64 = f32[2,256,128]{2,1,0:T(8,128)} custom-call(f32[2,512,4096]{2,1,0:T(8,128)} %sens.1, f32[2,512]{1,0:T(2,128)} %observed_in.1, f32[2,512]{1,0:T(2,128)} %noise_in.1, s32[2,512]{1,0:T(2,128)} %ids_in.1, f32[2,8,512]{2,1,0:T(8,128)} %perturb_in.1, f32[2,256,128]{2,1,0:T(8,128)} %bitcast.11), custom_call_target="tpu_custom_call" | custom-call | tf_op jit(solution)/shard_map/pallas_call | solution.py:389
  50.1 1.7 %copy.10 = f32[2,8,4,1024]{3,2,1,0:T(4,128)} copy(f32[2,8,4,1024]{3,2,1,0:T(4,128)} %bitcast.10) | data formatting | bytes 524288

commit v3 on v2

--- a/solution.py
+++ b/solution.py
@@ -14,6 +14,7 @@
 LANES = 128
 MODELS = 8
 PARTS = 1
+SLOTS = 3
 
 nu_value = 4.0
 step_size = 0.5
@@ -74,10 +75,12 @@
     order = sorted(range(layers), key=lambda l: 0 < l < layers - 1)
     pieces = [(l, slice(h * width, (h + 1) * width)) for l in order for h in range(PARTS)]
 
-    def load(s, l):
+    def load(n):
+        s, l = n // layers, lax.rem(n, layers)
+        slot = lax.rem(n, SLOTS)
         return pltpu.make_async_copy(
-            sens.at[s, :, pl.ds(pl.multiple_of(l * layer_cells, LANES), layer_cells)], raw.at[s, l],
-            load_sem.at[s, l],
+            sens.at[s, :, pl.ds(pl.multiple_of(l * layer_cells, LANES), layer_cells)], raw.at[slot],
+            load_sem.at[slot],
         )
 
     inputs = [
@@ -89,8 +92,8 @@
     ]
     for copy in inputs:
         copy.start()
-    for n in range(min(2, 2 * layers)):
-        load(n // layers, n % layers).start()
+    for n in range(SLOTS - 1):
+        load(jnp.int32(n)).start()
 
     barrier = pltpu.get_barrier_semaphore()
     pl.semaphore_signal(barrier, inc=1, device_id=(slab, me, partner), device_id_type=MESH)
@@ -343,14 +346,14 @@
 
         @pl.loop(0, layers)
         def _(l, s=s):
-            load(s, l).wait()
-            later = s * layers + l + 2
-
-            @pl.when(later < 2 * layers)
+            n = s * layers + l
+            load(n).wait()
+
+            @pl.when(n + SLOTS - 1 < 2 * layers)
             def _():
-                load(later // layers, lax.rem(later, layers)).start()
-
-            value = raw[s, l]
+                load(n + SLOTS - 1).start()
+
+            value = raw[lax.rem(n, SLOTS)]
             rounded = value.astype(jnp.bfloat16)
             high[s, l] = rounded
             low[s, l] = (value - rounded.astype(jnp.float32)).astype(jnp.bfloat16)
@@ -389,7 +392,7 @@
     out = pl.pallas_call(
         functools.partial(kernel, cells, layers),
         out_shape=jax.ShapeDtypeStruct(flat, f32),
-        in_specs=[pl.BlockSpec(memory_space=pl.ANY)] * 6,
+        in_specs=[pl.BlockSpec(memory_space=pltpu.HBM)] * 6,
         out_specs=pl.BlockSpec(memory_space=pl.ANY),
         scratch_shapes=[
             pltpu.VMEM((2, stations), f32),
@@ -400,7 +403,7 @@
             pltpu.VMEM(field, f32),
             pltpu.VMEM(field, f32),
             pltpu.VMEM(flat, f32),
-            pltpu.VMEM((2, layers, stations, layer_cells), f32),
+            pltpu.VMEM((SLOTS, stations, layer_cells), f32),
             pltpu.VMEM((2, layers, stations, layer_cells), bf16),
             pltpu.VMEM((2, layers, stations, layer_cells), bf16),
             pltpu.VMEM((2, layers, layer_cells, stations), bf16),
@@ -422,7 +425,7 @@
             pltpu.VMEM((ITERS, 2, pieces, models, width), f32),
             dma((5,)),
             dma((2,)),
-            dma((2, layers)),
+            dma((SLOTS,)),
             dma((2, 2)),
             dma((ITERS, 2, 2)),
             dma((2,)),
@@ -433,9 +436,9 @@
             dma((ITERS, 2, pieces)),
         ],
         compiler_params=pltpu.CompilerParams(
-            collective_id=0, has_side_effects=True, vmem_limit_bytes=57000 * 1024
+            collective_id=0, has_side_effects=True, vmem_limit_bytes=52000 * 1024
         ),
-    )(sens, observed, noise, survey_ids, data_perturb, prior)
+    )(*[pltpu.with_memory_space_constraint(x, pltpu.HBM) for x in (sens, observed, noise, survey_ids, data_perturb, prior)])
     out = out.reshape(2, models, blocks, layers, LANES).transpose(0, 1, 3, 2, 4)
     return out.reshape(2, models, layers, layer_cells)
 

time: 52 us -> 50.5 us (0.971)
  local copies, waits for them, and re-layouts: 1.67 us -> 0.71 us
    unnamed x1, local copies, waits for them, and re-layouts: 1.67 us -> 0.71 us
where the time goes in v3:
time: 50.5 us; the launch traced here: 50.4 us
  Pallas kernels  49.6 us (98%)
  local copies, waits for them, and re-layouts  0.71 us (1%)
    pallas_call x1, Pallas kernels, body(): pl.pallas_call(functools.partial(kernel, cells, layers), out_shape=jax.Sh...  49.6 us

profile of v3, /device:TPU:0, one launch (start us, length us, event | category | flops | bytes accessed | tf_op | source)
XLA Modules:
  0.0 50.4 jit_solution(820056563281281071)
XLA Ops:
  0.0 49.6 %shard_map.64 = f32[2,256,128]{2,1,0:T(8,128)S(1)} custom-call(f32[2,512,4096]{2,1,0:T(8,128)} %sens.1, f32[2,512]{1,0:T(2,128)} %observed_in.1, f32[2,512]{1,0:T(2,128)} %noise_in.1, s32[2,512]{1,0:T(2,128)} %ids_in.1, f32[2,8,512]{2,1,0:T(8,128)} %perturb_in.1, f32[2,256,128]{2,1,0:T(8,128)} %bitcast.11), custom_call_target="tpu_custom_call" | custom-call | tf_op jit(solution)/shard_map/pallas_call | solution.py:392
  49.7 0.7 %copy.10 = f32[2,8,4,1024]{3,2,1,0:T(4,128)} copy(f32[2,8,4,1024]{3,2,1,0:T(4,128)S(1)} %bitcast.10) | data formatting | bytes 524288

commit v4 on v3

--- a/solution.py
+++ b/solution.py
@@ -58,10 +58,10 @@
 
 
 def kernel(
-    cells, layers, sens, observed_in, noise_in, ids_in, perturb_in, prior_in, result_out,
-    observed, noise, survey_ids, perturb, prior_raw, prior, out, result, raw, high, low, high_t, low_t, base, carry_z, halo_up, halo_dn, acc, gather, target, per_noise, resids,
+    cells, layers, sens, observed_in, noise_in, ids_in, perturb_in, prior_in, result,
+    observed, noise, survey_ids, perturb, prior_raw, prior, out, raw, high, low, high_t, low_t, base, carry_z, halo_up, halo_dn, acc, gather, target, per_noise, resids,
     count_tile, sums_mine, sums_other, rows, grad_mine, grad_other,
-    input_sem, result_sem, load_sem, halo_send, halo_recv, part_send, part_recv, sums_send, sums_recv, grad_send, grad_recv,
+    input_sem, load_sem, halo_send, halo_recv, part_send, part_recv, sums_send, sums_recv, grad_send, grad_recv,
 ):
     stations = observed.shape[1]
     layer_cells = prior.shape[3]
@@ -312,8 +312,6 @@
         wait_parts_sent(it, s)
         if not last:
             send_parts(it + 1, s, total)
-        if last:
-            pltpu.make_async_copy(result.at[s], result_out.at[s], result_sem.at[s]).start()
         sums_copy(it, s).wait_send()
         for p in range(len(pieces)):
             grad_copy(it, s, p).wait_send()
@@ -370,8 +368,6 @@
             step(out, it, False)
     if ITERS > 1:
         step(out, ITERS - 1, True)
-    for s in range(2):
-        pltpu.make_async_copy(result.at[s], result_out.at[s], result_sem.at[s]).wait()
 
 
 def body(sens, observed, noise, survey_ids, data_perturb, prior):
@@ -393,7 +389,7 @@
         functools.partial(kernel, cells, layers),
         out_shape=jax.ShapeDtypeStruct(flat, f32),
         in_specs=[pl.BlockSpec(memory_space=pltpu.HBM)] * 6,
-        out_specs=pl.BlockSpec(memory_space=pl.ANY),
+        out_specs=vmem,
         scratch_shapes=[
             pltpu.VMEM((2, stations), f32),
             pltpu.VMEM((2, stations), f32),
@@ -402,7 +398,6 @@
             pltpu.VMEM(flat, f32),
             pltpu.VMEM(field, f32),
             pltpu.VMEM(field, f32),
-            pltpu.VMEM(flat, f32),
             pltpu.VMEM((SLOTS, stations, layer_cells), f32),
             pltpu.VMEM((2, layers, stations, layer_cells), bf16),
             pltpu.VMEM((2, layers, stations, layer_cells), bf16),
@@ -424,7 +419,6 @@
             pltpu.VMEM((2, pieces, models, width), f32),
             pltpu.VMEM((ITERS, 2, pieces, models, width), f32),
             dma((5,)),
-            dma((2,)),
             dma((SLOTS,)),
             dma((2, 2)),
             dma((ITERS, 2, 2)),

time: 50.5 us -> 50.3 us (level)
  no operation moved by 1% of the time
where the time goes in v4:
time: 50.3 us; the launch traced here: 50.1 us
  Pallas kernels  49.4 us (98%)
  local copies, waits for them, and re-layouts  0.71 us (1%)
    pallas_call x1, Pallas kernels, body(): pl.pallas_call(functools.partial(kernel, cells, layers), out_shape=jax.Sh...  49.4 us

profile of v4, /device:TPU:0, one launch (start us, length us, event | category | flops | bytes accessed | tf_op | source)
XLA Modules:
  0.0 50.1 jit_solution(18305086271198904917)
XLA Ops:
  0.0 49.4 %shard_map.64 = f32[2,256,128]{2,1,0:T(8,128)S(1)} custom-call(f32[2,512,4096]{2,1,0:T(8,128)} %sens.1, f32[2,512]{1,0:T(2,128)} %observed_in.1, f32[2,512]{1,0:T(2,128)} %noise_in.1, s32[2,512]{1,0:T(2,128)} %ids_in.1, f32[2,8,512]{2,1,0:T(8,128)} %perturb_in.1, f32[2,256,128]{2,1,0:T(8,128)} %bitcast.11), custom_call_target="tpu_custom_call" | custom-call | tf_op jit(solution)/shard_map/pallas_call | solution.py:388
  49.4 0.7 %copy.10 = f32[2,8,4,1024]{3,2,1,0:T(4,128)} copy(f32[2,8,4,1024]{3,2,1,0:T(4,128)S(1)} %bitcast.10) | data formatting | bytes 524288

commit v5 on v4

--- a/solution.py
+++ b/solution.py
@@ -329,8 +329,11 @@
                 couple_below(source, it)
 
         gradient(it, 0, beside)
+        if last:
+            residuals(it, 1)
         advance(source, it, 0, last)
-        residuals(it, 1)
+        if not last:
+            residuals(it, 1)
         weigh(it, 1)
         gradient(it, 1, lambda p: None)
         advance(source, it, 1, last)

time: 50.3 us -> 50.3 us (level)
  no operation moved by 1% of the time
where the time goes in v5:
time: 50.3 us; the launch traced here: 50.1 us
  Pallas kernels  49.4 us (98%)
  local copies, waits for them, and re-layouts  0.71 us (1%)
    pallas_call x1, Pallas kernels, body(): pl.pallas_call(functools.partial(kernel, cells, layers), out_shape=jax.Sh...  49.4 us

profile of v5, /device:TPU:0, one launch (start us, length us, event | category | flops | bytes accessed | tf_op | source)
XLA Modules:
  0.0 50.1 jit_solution(17138859517224079010)
XLA Ops:
  0.0 49.4 %shard_map.64 = f32[2,256,128]{2,1,0:T(8,128)S(1)} custom-call(f32[2,512,4096]{2,1,0:T(8,128)} %sens.1, f32[2,512]{1,0:T(2,128)} %observed_in.1, f32[2,512]{1,0:T(2,128)} %noise_in.1, s32[2,512]{1,0:T(2,128)} %ids_in.1, f32[2,8,512]{2,1,0:T(8,128)} %perturb_in.1, f32[2,256,128]{2,1,0:T(8,128)} %bitcast.11), custom_call_target="tpu_custom_call" | custom-call | tf_op jit(solution)/shard_map/pallas_call | solution.py:391
  49.4 0.7 %copy.10 = f32[2,8,4,1024]{3,2,1,0:T(4,128)} copy(f32[2,8,4,1024]{3,2,1,0:T(4,128)S(1)} %bitcast.10) | data formatting | bytes 524288
